TPU v7x, 512 devices: a whole 4x4x16 slice. The times are simulated.
512 devices in a mesh: seq: 32 (over z, core), heads: 4 (over x), dp: 4 (over y).
Axes of the slice: x: 4, y: 4, z: 16, core: 2. Of those that a mesh axis runs over, the one named last changes fastest.
Arguments:
- tokens: bfloat16 [4, 4096, 3072], P('dp', 'seq'), may hold values from -6 to 6
- proj_weights: bfloat16 [3, 3072, 4096], P(None, 'seq', ('heads', 'dp')), may hold values from -0.109375 to 0.109375
- norm_gain: float32 [4096], P(('heads', 'dp')), may hold values from 0.5 to 1.5
Outputs:
- attended: bfloat16 [4, 4096, 4096], P('dp', 'seq', 'heads')
All inputs are finite; a program needn't handle non-finite values.
Results may differ from a plain program's by a relative error of at most 0.0063.
Values may be sent and summed in bfloat16 or wider, within the bound.
No kernel may reach another device: no remote copies, remote signals or barrier semaphores. Data moves between devices by JAX's collectives and lax.ppermute only.
A program may use at most 64 MiB of HBM per device.

v0:
```python
import jax
import jax.numpy as jnp
from jax import lax
from jax.sharding import PartitionSpec as P

DH = 128


def prefix_2(part, axis, combine, identity):
    place = lax.axis_index(axis)
    gathered = lax.all_gather(part, axis)
    state = jnp.zeros_like(part) + jnp.asarray(identity, part.dtype)

    def one(step, state):
        return combine(state, lax.dynamic_index_in_dim(gathered, step, 0, False))

    return lax.fori_loop(0, place, one, state)


def add_pair(earlier, later):
    return earlier + later


def project_rows(flat_rows):

    def accumulate(total, piece, start):
        return jnp.einsum("nd,jdc->jnc", flat_rows, piece, preferred_element_type=jnp.float32)

    return accumulate


def to_heads(matrix, seq_count, length):
    return matrix.reshape(seq_count, length, -1, DH)


def activate(matrix, seq_count, length):
    return to_heads(jax.nn.silu(matrix).astype(jnp.bfloat16), seq_count, length)


def block_prefix(keys_b, values_b):
    state = jnp.einsum("sthd,sthe->shde", keys_b, values_b, preferred_element_type=jnp.float32)
    return prefix_2(state, "seq", add_pair, jnp.zeros_like(state))


def attend(queries, keys_b, values_b, prefix, norm_gain):
    seq_count, length, head_count, head_size = queries.shape
    scores = jnp.einsum("sthd,suhd->shtu", queries, keys_b, preferred_element_type=jnp.float32)
    causal = lax.broadcasted_iota(jnp.int32, (length, length), 0) >= lax.broadcasted_iota(
        jnp.int32, (length, length), 1
    )
    scores_b = jnp.where(causal, scores, 0.0).astype(jnp.bfloat16)
    local = jnp.einsum("shtu,suhd->sthd", scores_b, values_b, preferred_element_type=jnp.float32)
    carried = jnp.einsum(
        "sthd,shde->sthe", queries, prefix.astype(jnp.bfloat16), preferred_element_type=jnp.float32
    )
    attn = local + carried
    scale = lax.rsqrt(jnp.mean(attn * attn, axis=-1, keepdims=True) + 1e-06)
    normed = attn * scale * norm_gain.reshape(head_count, head_size)
    return normed.astype(jnp.bfloat16).reshape(seq_count, length, head_count * head_size)


def body(tokens, proj_weights, norm_gain):
    everyone = lax.all_gather(tokens, "dp", axis=0, tiled=True)
    seq_count, length, width = everyone.shape
    total_rows = seq_count * length
    per_device = proj_weights.shape[2]
    accumulate = project_rows(everyone.reshape(total_rows, width))
    start_sum = jnp.zeros((3, total_rows, per_device), jnp.float32)
    projected = accumulate(
        start_sum, lax.all_gather(proj_weights, "seq", axis=1, tiled=True), jnp.int32(0)
    )
    queries = activate(projected[0], seq_count, length)
    keys_b = activate(projected[1], seq_count, length)
    values_b = to_heads(projected[2].astype(jnp.bfloat16), seq_count, length)
    prefix = block_prefix(keys_b, values_b)
    normed = attend(queries, keys_b, values_b, prefix, norm_gain)
    return lax.all_to_all(normed, "dp", split_axis=0, concat_axis=2, tiled=True)


def solution(mesh):
    in_specs = (P("dp", "seq", None), P(None, "seq", ("heads", "dp")), P(("heads", "dp")))
    out_specs = P("dp", "seq", "heads")
    return jax.shard_map(body, mesh=mesh, in_specs=in_specs, out_specs=out_specs, check_vma=False)
```

profile of v0, /device:TPU:481, one launch (start us, length us, event | category | flops | bytes accessed | tf_op | source)
XLA Modules:
  0.0 297.7 jit_solution(694654217346947341)
XLA Ops:
  8.1 47.7 %all-gather.7.cloned.1.call-done = bf16[4,128,3072]{2,1,0:T(8,128)(2,1)} async-done(((bf16[1,128,3072]{2,1,0:T(8,128)(2,1)}), bf16[4,128,3072]{2,1,0:T(8,128)(2,1)}) %all-gather.7.cloned.1.call-update) | async-done | bytes 3145744 | tf_op jit(solution)/shard_map/all_gather | solution.py:63
  55.8 76.4 %all-gather.5.cloned.1.call-done = bf16[3,3072,256]{2,1,0:T(8,128)(2,1)} async-done(((bf16[3,96,256]{2,1,0:T(8,128)(2,1)}), bf16[3,3072,256]{2,1,0:T(8,128)(2,1)}) %all-gather.5.cloned.1.call-update) | async-done | bytes 4718608 | tf_op jit(solution)/shard_map/all_gather | solution.py:70
  132.1 5.5 %convolution_bitcast_fusion = f32[3,512,256]{1,2,0:T(8,128)S(1)} fusion(bf16[3,3072,256]{2,1,0:T(8,128)(2,1)} %all-gather.5.cloned.1.call-done, bf16[512,3072,1]{1,0,2:T(8,128)(2,1)} %bitcast.33), kind=kOutput, calls=%fused_computation.1 | convolution fusion | flops 2415919104 | bytes 9437184 | tf_op jit(solution)/shard_map/nd,jdc->jnc/dot_general | solution.py:27
  140.6 101.5 %all-gather.9.cloned.1.call-done = f32[128,2,128,128]{3,2,1,0:T(8,128)} async-done(((f32[4,2,128,128]{3,2,1,0:T(8,128)}), f32[128,2,128,128]{3,2,1,0:T(8,128)}) %all-gather.9.cloned.1.call-update) | async-done | bytes 16777232 | tf_op jit(solution)/shard_map/all_gather | solution.py:11
  242.2 37.0 %while.10 = (s32[]{:T(128)}, f32[4,2,128,128]{3,2,1,0:T(8,128)S(1)}, s32[]{:T(128)}, f32[32,4,2,128,128]{4,3,2,1,0:T(8,128)}, s32[]{:T(128)}, /*index=5*/s32[]{:T(128)}, s32[]{:T(128)}) while((s32[]{:T(128)}, f32[4,2,128,128]{3,2,1,0:T(8,128)S(1)}, s32[]{:T(128)}, f32[32,4,2,128,128]{4,3,2,1,0:T(8,128)}, s32[]{:T(128)}, /*index=5*/s32[]{:T(128)}, ...), condition=%wide.region_1.2_spmd, body=%wide.region_0.1_spmd.sunk | while | flops 131077 | bytes 1572987 | solution.py:17
  242.2 1.2 bitcast_add_fusion.2
  243.4 1.2 bitcast_add_fusion.2
  244.6 1.2 bitcast_add_fusion.2
  245.8 1.2 bitcast_add_fusion.2
  247.0 1.2 bitcast_add_fusion.2
  248.2 1.2 bitcast_add_fusion.2
  249.3 1.2 bitcast_add_fusion.2
  250.5 1.2 bitcast_add_fusion.2
  251.7 1.2 bitcast_add_fusion.2
  252.9 1.2 bitcast_add_fusion.2
  254.1 1.2 bitcast_add_fusion.2
  255.3 1.2 bitcast_add_fusion.2
  256.5 1.2 bitcast_add_fusion.2
  257.7 1.2 bitcast_add_fusion.2
  258.9 1.2 bitcast_add_fusion.2
  260.1 1.2 bitcast_add_fusion.2
  263.7 1.2 bitcast_add_fusion.2
  264.9 1.2 bitcast_add_fusion.2
  266.0 1.2 bitcast_add_fusion.2
  267.2 1.2 bitcast_add_fusion.2
  268.4 1.2 bitcast_add_fusion.2
  269.6 1.2 bitcast_add_fusion.2
  274.4 1.2 bitcast_add_fusion.2
  275.6 1.2 bitcast_add_fusion.2
  276.8 1.2 bitcast_add_fusion.2
  278.0 1.2 bitcast_add_fusion.2
  279.7 10.6 %all_to_all.18 = bf16[4,128,256]{1,2,0:T(8,128)(2,1)S(1)} all-to-all(bf16[4,128,256]{1,2,0:T(8,128)(2,1)S(1)} %bitcast.29), channel_id=1, replica_groups=mesh['seq'=32,'heads'=4,'dp'=4] {'dp'}, dimensions={0} | all-to-all | bytes 524288 | tf_op jit(solution)/shard_map/all_to_all | solution.py:77
  (29 shorter events, 11.6 us)
Async XLA Ops:
  6.5 49.2 %all-gather.7.cloned.1.call-start = ((), (), s32[]{:S(2)}) async-start(), calls=%async_computation.2 | async-start | bytes 3932160 | tf_op jit(solution)/shard_map/all_gather | solution.py:63
  7.3 124.9 %all-gather.5.cloned.1.call-start = ((), (), s32[]{:S(2)}) async-start(), calls=%async_computation.1 | async-start | bytes 4866048 | tf_op jit(solution)/shard_map/all_gather | solution.py:70
  8.0 234.1 %all-gather.9.cloned.1.call-start = ((), (), s32[]{:S(2)}) async-start(), calls=%async_computation.3 | async-start | bytes 17301504 | tf_op jit(solution)/shard_map/all_gather | solution.py:11
  242.1 37.4 %copy-start = (f32[256]{0:T(256)S(1)}, f32[256]{0:T(256)}, u32[]{:S(2)}) copy-start(f32[256]{0:T(256)} %param.7) | copy-start | bytes 3076
Sparse Core Ops, SparseCore 0:
  9.5 46.2 all-gather.6
  57.9 74.1 all-gather.4
  139.7 102.3 all-gather.8
where the time goes:
time: 299 us; the launch traced here: 298 us
  waiting for transfers between devices  227 us (76%)
  other arithmetic  36.4 us (12%)
  between operations  13.2 us (4%)
  blocking collectives  10.6 us (4%)
  matrix products  7.57 us (3%)
    all_gather x1, waiting for transfers between devices, prefix_2(): gathered = lax.all_gather(part, axis)  101 us
    all_gather x1, waiting for transfers between devices, body(): lax.all_gather(proj_weights, 'seq', axis=1, tiled=True)  76.4 us
    all_gather x1, waiting for transfers between devices, body(): everyone = lax.all_gather(tokens, 'dp', axis=0, tiled=True)  47.7 us
    add x31, other arithmetic, add_pair(): return earlier + later  36.3 us
    all_to_all x1, blocking collectives, body(): return lax.all_to_all(normed, 'dp', split_axis=0, concat_axis=2, tiled=True)  10.6 us
  transfers between devices with their start and end apart: 3, of which 3 were waited for; matrix products, arithmetic and copies ran while one was open for 0% of the time, Pallas kernels for 0%

commit v1 on v0

--- a/solution.py
+++ b/solution.py
@@ -60,7 +60,24 @@
 
 
 def body(tokens, proj_weights, norm_gain):
-    everyone = lax.all_gather(tokens, "dp", axis=0, tiled=True)
+    peers, index, width_2 = (lax.axis_size("dp"), lax.axis_index("dp"), tokens.shape[0])
+    right = [(i, (i + 1) % peers) for i in range(peers)]
+    backward = [(i, (i - 1) % peers) for i in range(peers)]
+    out = jnp.zeros((*tokens.shape[:0], peers * width_2, *tokens.shape[0 + 1 :]), tokens.dtype)
+    out = lax.dynamic_update_slice_in_dim(out, tokens, index * width_2, axis=0)
+    from_left = from_right = tokens
+    halfway = peers // 2
+    for step_2 in range(1, halfway + 1):
+        from_left = lax.ppermute(from_left, "dp", right)
+        out = lax.dynamic_update_slice_in_dim(
+            out, from_left, (index - step_2) % peers * width_2, axis=0
+        )
+        if step_2 < peers - halfway:
+            from_right = lax.ppermute(from_right, "dp", backward)
+            out = lax.dynamic_update_slice_in_dim(
+                out, from_right, (index + step_2) % peers * width_2, axis=0
+            )
+    everyone = out
     seq_count, length, width = everyone.shape
     total_rows = seq_count * length
     per_device = proj_weights.shape[2]

time: 299 us -> 249 us (0.83)
  waiting for transfers between devices: 227 us -> 165 us
  starting transfers between devices: 0.08 us -> 8.52 us
  local copies, waits for them, and re-layouts: 2.07 us -> 5.68 us
    all_gather x1 -> x0, waiting for transfers between devices: 47.7 us -> none  [body(): everyone = lax.all_gather(tokens, 'dp', axis=0, tiled=True)]
    all_gather x1, waiting for transfers between devices: 76.4 us -> 31 us  [body(): lax.all_gather(proj_weights, 'seq', axis=1, tiled=True)]
    ppermute x0 -> x3, waiting for transfers between devices: none -> 31.5 us  [the longest x2 31.5 us: body(): from_left = lax.ppermute(from_left, 'dp', right)]
    ppermute x0 -> x3, starting transfers between devices: none -> 8.48 us  [the longest x2 5.12 us: body(): from_left = lax.ppermute(from_left, 'dp', right)]
    dynamic_update_slice x0 -> x4, local copies, waits for them, and re-layouts: none -> 3.71 us  [the longest x2 2.42 us: body(): lax.dynamic_update_slice_in_dim(out, from_left, (index - step_2) % peers...]
  transfers between devices with their start and end apart: 3 -> 5, of which waited for: 3 -> 4; matrix products, arithmetic and copies ran while one was open for 0% -> 2% of each run, Pallas kernels for 0% -> 0%
where the time goes in v1:
time: 249 us; the launch traced here: 247 us
  waiting for transfers between devices  165 us (66%)
  other arithmetic  36.4 us (15%)
  between operations  13.6 us (5%)
  blocking collectives  10.6 us (4%)
  starting transfers between devices  8.52 us (3%)
  matrix products  7 us (3%)
  local copies, waits for them, and re-layouts  5.68 us (2%)
    all_gather x1, waiting for transfers between devices, prefix_2(): gathered = lax.all_gather(part, axis)  102 us
    add x31, other arithmetic, add_pair(): return earlier + later  36.3 us
    ppermute x2, waiting for transfers between devices, body(): from_left = lax.ppermute(from_left, 'dp', right)  31.5 us
    all_gather x1, waiting for transfers between devices, body(): lax.all_gather(proj_weights, 'seq', axis=1, tiled=True)  31 us
    all_to_all x1, blocking collectives, body(): return lax.all_to_all(normed, 'dp', split_axis=0, concat_axis=2, tiled=True)  10.6 us
    ppermute x2, starting transfers between devices, body(): from_left = lax.ppermute(from_left, 'dp', right)  5.12 us
  transfers between devices with their start and end apart: 5, of which 4 were waited for; matrix products, arithmetic and copies ran while one was open for 2% of the time, Pallas kernels for 0%

profile of v1, /device:TPU:481, one launch (start us, length us, event | category | flops | bytes accessed | tf_op | source)
XLA Modules:
  0.0 247.5 jit_solution(10622822817110883523)
XLA Ops:
  7.3 3.2 %collective-permute-start = (bf16[1,128,3072]{2,1,0:T(8,128)(2,1)}, bf16[1,128,3072]{2,1,0:T(8,128)(2,1)}, u32[]{:S(2)}, u32[]{:S(2)}) collective-permute-start(bf16[1,128,3072]{2,1,0:T(8,128)(2,1)} %param.5), channel_id=1, source_target_pairs={{0,1},{1,2},{2,3},{3,0},{4,5},{5,6},{6,7},{7,4},{8,9},{9,10},{10,1... | collective-permute-start | bytes 2359304 | tf_op jit(solution)/shard_map/ppermute | solution.py:71
  10.5 3.4 %collective-permute-start.1 = (bf16[1,128,3072]{2,1,0:T(8,128)(2,1)}, bf16[1,128,3072]{2,1,0:T(8,128)(2,1)}, u32[]{:S(2)}, u32[]{:S(2)}) collective-permute-start(bf16[1,128,3072]{2,1,0:T(8,128)(2,1)} %param.5), channel_id=1, source_target_pairs={{0,3},{1,0},{2,1},{3,2},{4,7},{5,4},{6,5},{7,6},{8,11},{9,8},{10,9... | collective-permute-start | bytes 2359304 | tf_op jit(solution)/shard_map/ppermute | solution.py:76
  13.9 15.4 %collective-permute-done = bf16[1,128,3072]{2,1,0:T(8,128)(2,1)} collective-permute-done((bf16[1,128,3072]{2,1,0:T(8,128)(2,1)}, bf16[1,128,3072]{2,1,0:T(8,128)(2,1)}, u32[]{:S(2)}, u32[]{:S(2)}) %collective-permute-start) | collective-permute-done | bytes 786464 | tf_op jit(solution)/shard_map/ppermute | solution.py:71
  29.3 1.9 collective-permute-start.2
  31.7 1.2 constant_dynamic-update-slice_fusion.2
  33.0 1.2 constant_dynamic-update-slice_fusion.1
  34.2 16.1 %collective-permute-done.2 = bf16[1,128,3072]{2,1,0:T(8,128)(2,1)} collective-permute-done((bf16[1,128,3072]{2,1,0:T(8,128)(2,1)}, bf16[1,128,3072]{2,1,0:T(8,128)(2,1)}, u32[]{:S(2)}, u32[]{:S(2)}) %collective-permute-start.2) | collective-permute-done | bytes 786464 | tf_op jit(solution)/shard_map/ppermute | solution.py:71
  50.3 1.2 constant_dynamic-update-slice_fusion
  51.5 31.0 %all-gather.4.cloned.1.call-done = bf16[3,3072,256]{2,1,0:T(8,128)(2,1)} async-done(((bf16[3,96,256]{2,1,0:T(8,128)(2,1)}), bf16[3,3072,256]{2,1,0:T(8,128)(2,1)}) %all-gather.4.cloned.1.call-update) | async-done | bytes 4718608 | tf_op jit(solution)/shard_map/all_gather | solution.py:87
  82.5 4.9 %convolution_bitcast_fusion = f32[3,512,256]{2,1,0:T(8,128)S(1)} fusion(bf16[512,3072,1]{1,0,2:T(8,128)(2,1)S(1)} %bitcast.21, bf16[3,3072,256]{2,1,0:T(8,128)(2,1)} %all-gather.4.cloned.1.call-done), kind=kOutput, calls=%fused_computation.1 | convolution fusion | flops 2415919104 | bytes 9437184 | tf_op jit(solution)/shard_map/nd,jdc->jnc/dot_general | solution.py:27
  89.9 101.7 %all-gather.6.cloned.1.call-done = f32[128,2,128,128]{3,2,1,0:T(8,128)} async-done(((f32[4,2,128,128]{3,2,1,0:T(8,128)}), f32[128,2,128,128]{3,2,1,0:T(8,128)}) %all-gather.6.cloned.1.call-update) | async-done | bytes 16777232 | tf_op jit(solution)/shard_map/all_gather | solution.py:11
  191.6 37.0 %while.10 = (s32[]{:T(128)}, f32[4,2,128,128]{3,2,1,0:T(8,128)S(1)}, s32[]{:T(128)}, f32[32,4,2,128,128]{4,3,2,1,0:T(8,128)}, s32[]{:T(128)}, /*index=5*/s32[]{:T(128)}, s32[]{:T(128)}) while((s32[]{:T(128)}, f32[4,2,128,128]{3,2,1,0:T(8,128)S(1)}, s32[]{:T(128)}, f32[32,4,2,128,128]{4,3,2,1,0:T(8,128)}, s32[]{:T(128)}, /*index=5*/s32[]{:T(128)}, ...), condition=%wide.region_1.2_spmd, body=%wide.region_0.1_spmd.sunk | while | flops 131077 | bytes 1572987 | solution.py:17
  192.9 1.2 bitcast_add_fusion.2
  194.1 1.2 bitcast_add_fusion.2
  195.2 1.2 bitcast_add_fusion.2
  196.4 1.2 bitcast_add_fusion.2
  197.6 1.2 bitcast_add_fusion.2
  198.8 1.2 bitcast_add_fusion.2
  204.8 1.2 bitcast_add_fusion.2
  206.0 1.2 bitcast_add_fusion.2
  207.2 1.2 bitcast_add_fusion.2
  208.4 1.2 bitcast_add_fusion.2
  209.6 1.2 bitcast_add_fusion.2
  210.8 1.2 bitcast_add_fusion.2
  215.5 1.2 bitcast_add_fusion.2
  216.7 1.2 bitcast_add_fusion.2
  217.9 1.2 bitcast_add_fusion.2
  219.1 1.2 bitcast_add_fusion.2
  220.3 1.2 bitcast_add_fusion.2
  221.5 1.2 bitcast_add_fusion.2
  227.5 1.2 bitcast_add_fusion.2
  229.2 10.6 %all_to_all.18 = bf16[4,128,256]{1,2,0:T(8,128)(2,1)S(1)} all-to-all(bf16[4,128,256]{1,2,0:T(8,128)(2,1)S(1)} %bitcast.22), channel_id=1, replica_groups=mesh['seq'=32,'heads'=4,'dp'=4] {'dp'}, dimensions={0} | all-to-all | bytes 524288 | tf_op jit(solution)/shard_map/all_to_all | solution.py:94
  (36 shorter events, 19.1 us)
Async XLA Ops:
  6.5 75.9 %all-gather.4.cloned.1.call-start = ((), (), s32[]{:S(2)}) async-start(), calls=%async_computation.1 | async-start | bytes 4866048 | tf_op jit(solution)/shard_map/all_gather | solution.py:87
  7.3 184.3 %all-gather.6.cloned.1.call-start = ((), (), s32[]{:S(2)}) async-start(), calls=%async_computation.2 | async-start | bytes 17301504 | tf_op jit(solution)/shard_map/all_gather | solution.py:11
  7.3 22.0 %collective-permute-start = (bf16[1,128,3072]{2,1,0:T(8,128)(2,1)}, bf16[1,128,3072]{2,1,0:T(8,128)(2,1)}, u32[]{:S(2)}, u32[]{:S(2)}) collective-permute-start(bf16[1,128,3072]{2,1,0:T(8,128)(2,1)} %param.5), channel_id=1, source_target_pairs={{0,1},{1,2},{2,3},{3,0},{4,5},{5,6},{6,7},{7,4},{8,9},{9,10},{10,1... | collective-permute-start | bytes 2359304 | tf_op jit(solution)/shard_map/ppermute | solution.py:71
  10.5 22.4 %collective-permute-start.1 = (bf16[1,128,3072]{2,1,0:T(8,128)(2,1)}, bf16[1,128,3072]{2,1,0:T(8,128)(2,1)}, u32[]{:S(2)}, u32[]{:S(2)}) collective-permute-start(bf16[1,128,3072]{2,1,0:T(8,128)(2,1)} %param.5), channel_id=1, source_target_pairs={{0,3},{1,0},{2,1},{3,2},{4,7},{5,4},{6,5},{7,6},{8,11},{9,8},{10,9... | collective-permute-start | bytes 2359304 | tf_op jit(solution)/shard_map/ppermute | solution.py:76
  13.9 17.7 %copy-start = (bf16[1,128,3072]{2,1,0:T(8,128)(2,1)S(1)}, bf16[1,128,3072]{2,1,0:T(8,128)(2,1)}, u32[]{:S(2)}) copy-start(bf16[1,128,3072]{2,1,0:T(8,128)(2,1)} %param.5) | copy-start | bytes 2359300
  29.3 21.0 %collective-permute-start.2 = (bf16[1,128,3072]{2,1,0:T(8,128)(2,1)}, bf16[1,128,3072]{2,1,0:T(8,128)(2,1)}, u32[]{:S(2)}, u32[]{:S(2)}) collective-permute-start(bf16[1,128,3072]{2,1,0:T(8,128)(2,1)} %collective-permute-done), channel_id=1, source_target_pairs={{0,1},{1,2},{2,3},{3,0},{4,5},{5,6},{6,7},{7,4},{8,9},{9,10},{10,1... | collective-permute-start | bytes 2359304 | tf_op jit(solution)/shard_map/ppermute | solution.py:71
  191.6 37.4 %copy-start.1 = (f32[256]{0:T(256)S(1)}, f32[256]{0:T(256)}, u32[]{:S(2)}) copy-start(f32[256]{0:T(256)} %param.7) | copy-start | bytes 3076
Sparse Core Ops, SparseCore 0:
  9.5 72.9 all-gather.3
  89.1 102.3 all-gather.5
